TPU v7x, 32 devices: a whole 2x2x4 slice. The times are simulated.
32 devices in a mesh: dp: 8 (over z, x), tensor: 4 (over y, core).
Axes of the slice: x: 2, y: 2, z: 4, core: 2. Of those that a mesh axis runs over, the one named last changes fastest.
Arguments:
- context: bfloat16 [2, 8192, 3072], P(None, 'dp', 'tensor'), may hold values from -6 to 6
- out_grad: bfloat16 [2, 8192, 3072], P(None, ('dp', 'tensor')), may hold values from -0.1875 to 0.1875
- error_in: bfloat16 [2, 24576, 3072], P(None, 'dp', 'tensor'), may hold values from -6 to 6
- right_init: float32 [2, 64, 3072], P(None, None, 'tensor'), may hold values from -6 to 6
Outputs:
- summed_update: bfloat16 [2, 3072, 3072], P(None, 'dp', 'tensor')
- error_out: bfloat16 [2, 24576, 3072], P(None, 'dp', 'tensor')
All inputs are finite; a program needn't handle non-finite values.
Results may differ from a plain program's by a relative error of at most 0.015.
Values may be sent and summed in bfloat16 or wider, within the bound.
A program may use at most 128 MiB of HBM per device.

v0:
```python
import jax
import jax.numpy as jnp
from jax import lax
from jax.sharding import PartitionSpec as P


def solve_rows(gram_matrix, left_factor):
    ridge_term = 1e-06 * jnp.mean(jnp.diagonal(gram_matrix, axis1=1, axis2=2), axis=1)
    eye_matrix = jnp.eye(gram_matrix.shape[1], dtype=gram_matrix.dtype)
    gram_matrix = gram_matrix + ridge_term[:, None, None] * eye_matrix
    factor_low = jnp.linalg.cholesky(gram_matrix)

    def one_solve(low_part, rhs_part):
        return jax.scipy.linalg.solve_triangular(low_part, rhs_part, lower=True)

    return jax.vmap(one_solve)(factor_low, left_factor)


def gram_of(left_factor):
    return jnp.einsum("lrd,lsd->lrs", left_factor, left_factor, precision=lax.Precision.HIGHEST)


def compress(context, out_grad, error_in, right_init):
    out_width = out_grad.shape[2]
    moment = jnp.einsum(
        "ltd,lte->lde",
        lax.all_gather(out_grad, "tensor", axis=1, tiled=True),
        context,
        preferred_element_type=jnp.float32,
    )
    moment = moment + error_in.astype(jnp.float32)
    left_factor = jnp.einsum("lre,lde->lrd", right_init, moment, precision=lax.Precision.HIGHEST)
    left_part = lax.psum_scatter(left_factor, "tensor", scatter_dimension=2, tiled=True)
    left_part = lax.psum(left_part, "dp")
    gram_matrix = lax.psum(gram_of(left_part), "tensor")
    ortho_part = solve_rows(gram_matrix, left_part)
    ortho_basis = lax.all_gather(ortho_part, "tensor", axis=2, tiled=True)
    right_terms = jnp.einsum("lrd,lde->lre", ortho_basis, moment, precision=lax.Precision.HIGHEST)
    right_factor = lax.psum(right_terms.astype(jnp.bfloat16), "dp").astype(jnp.float32)
    replicas = lax.axis_size("dp")
    row_share = out_width // replicas
    own_basis = lax.dynamic_slice_in_dim(
        ortho_basis, lax.axis_index("dp") * row_share, row_share, 2
    )
    summed = jnp.einsum("lrd,lre->lde", own_basis, right_factor, precision=lax.Precision.HIGHEST)
    mean_part = jnp.einsum(
        "lrd,lre->lde", ortho_basis, right_factor / replicas, precision=lax.Precision.HIGHEST
    )
    new_error = (moment - mean_part).astype(jnp.bfloat16)
    return (summed.astype(jnp.bfloat16), new_error)


def body(context, out_grad, error_in, right_init):
    return compress(context, out_grad, error_in, right_init)


def solution(mesh):
    return jax.shard_map(
        body,
        mesh=mesh,
        in_specs=(
            P(None, "dp", "tensor"),
            P(None, ("dp", "tensor"), None),
            P(None, "dp", "tensor"),
            P(None, None, "tensor"),
        ),
        out_specs=(P(None, "dp", "tensor"), P(None, "dp", "tensor")),
        check_vma=False,
    )
```

profile of v0, /device:TPU:0, one launch (start us, length us, event | category | flops | bytes accessed | tf_op | source)
XLA Modules:
  0.0 419.1 jit_solution(9212171889300298580)
XLA Ops:
  7.2 4.8 %copy.12 = bf16[2,256,3072]{1,2,0:T(8,128)(2,1)} copy(bf16[2,256,3072]{2,1,0:T(8,128)(2,1)} %param.5) | data formatting | bytes 6291456 | tf_op args[1]
  12.1 86.6 %all-gather.3.cloned.1.call-done = bf16[2,1024,3072]{1,2,0:T(8,128)(2,1)} async-done(((bf16[2,256,3072]{1,2,0:T(8,128)(2,1)}), bf16[2,1024,3072]{1,2,0:T(8,128)(2,1)}) %all-gather.3.cloned.1.call-update) | async-done | bytes 12582928 | tf_op jit(solution)/shard_map/all_gather | solution.py:27
  98.7 19.3 %convert_add_fusion = f32[2,3072,768]{2,1,0:T(8,128)} fusion(bf16[2,3072,768]{2,1,0:T(8,128)(2,1)} %param.6, bf16[2,1024,3072]{1,2,0:T(8,128)(2,1)} %all-gather.3.cloned.1.call-done, bf16[2,1024,768]{2,1,0:T(8,128)(2,1)S(1)} %copy-done), kind=kOutput, calls=%fused_computation.2 | convolution fusion | flops 9673113600 | bytes 44040192 | tf_op jit(solution)/shard_map/ltd,lte->lde/dot_general | solution.py:25
  118.0 22.5 %convolution_bitcast_fusion = f32[2,64,3072]{2,1,0:T(8,128)} fusion(f32[2,3072,768]{2,1,0:T(8,128)} %convert_add_fusion, f32[2,64,768]{2,1,0:T(8,128)S(1)} %copy-done.4), kind=kOutput, calls=%fused_computation.3 | convolution fusion | flops 3623878656 | bytes 20840448 | tf_op jit(solution)/shard_map/lre,lde->lrd/dot_general | solution.py:32
  140.5 28.1 %reduce-scatter.2.cloned.1.call-done = f32[2,64,768]{2,1,0:T(8,128)} async-done(((f32[2,64,3072]{2,1,0:T(8,128)}), f32[2,64,768]{2,1,0:T(8,128)}) %reduce-scatter.2.cloned.1.call-update) | async-done | bytes 393232 | tf_op jit(solution)/shard_map/reduce_scatter | solution.py:33
  168.7 0.1 copy.15
  168.9 75.0 %all-reduce.3.cloned.1.call-done = f32[2,64,768]{2,1,0:T(8,128)} async-done(((f32[2,64,768]{2,1,0:T(8,128)}), f32[2,64,768]{2,1,0:T(8,128)}) %all-reduce.3.cloned.1.call-update) | async-done | bytes 393232 | tf_op jit(solution)/shard_map/psum | solution.py:34
  243.9 1.7 fusion.10
  245.5 10.9 %psum.22 = f32[2,64,64]{1,2,0:T(8,128)S(1)} all-reduce(f32[2,64,64]{1,2,0:T(8,128)S(1)} %fusion.10), channel_id=1, replica_groups=mesh['dp'=8,'tensor'=4] {'tensor'}, use_global_device_ids=true, to_apply=%region_2.0 | all-reduce | flops 8192 | bytes 65536 | tf_op jit(solution)/shard_map/psum | solution.py:35
  256.4 1.9 copy.14
  258.3 0.9 gather_fusion
  259.3 0.1 multiply_add_fusion
  259.3 0.1 copy.16
  259.4 0.1 fusion.6
  259.5 11.7 %custom-call.8 = f32[2,64,64]{2,1,0:T(8,128)S(1)} custom-call(f32[2,64,64]{2,1,0:T(8,128)S(1)} %fusion.6), custom_call_target="Cholesky" | custom-call | tf_op jit(solution)/shard_map/jit(cholesky)/cholesky | solution.py:11
  271.3 0.1 compare_reduce_fusion
  271.4 0.1 select_bitcast_fusion
  271.5 9.8 %custom-call.9 = f32[2,1,64,64]{2,3,1,0:T(8,128)S(1)} custom-call(f32[2,1,64,64]{3,2,1,0:T(8,128)S(1)} %select_bitcast_fusion), custom_call_target="InvertDiagBlocksLowerTriangular" | custom-call | tf_op jit(solution)/shard_map/vmap(jit(_solve_triangular))/triangular_solve | solution.py:14
  281.3 1.3 fusion.4
  282.7 18.8 %all-gather.5.cloned.1.call-done = f32[2,64,3072]{2,1,0:T(8,128)} async-done(((f32[2,64,768]{2,1,0:T(8,128)}), f32[2,64,3072]{2,1,0:T(8,128)}) %all-gather.5.cloned.1.call-update) | async-done | bytes 1572880 | tf_op jit(solution)/shard_map/all_gather | solution.py:37
  301.5 16.3 %convolution_convert_fusion.1 = bf16[2,64,768]{2,1,0:T(8,128)(2,1)} fusion(f32[2,64,3072]{2,1,0:T(8,128)} %all-gather.5.cloned.1.call-done, f32[2,3072,768]{2,1,0:T(8,128)} %convert_add_fusion), kind=kOutput, calls=%fused_computation.5 | convolution fusion | flops 3623976960 | bytes 20643840 | tf_op jit(solution)/shard_map/lrd,lde->lre/dot_general | solution.py:38
  317.8 70.8 %all-reduce.5.cloned.1.call-done = bf16[2,64,768]{2,1,0:T(8,128)(2,1)} async-done(((bf16[2,64,768]{2,1,0:T(8,128)(2,1)}), bf16[2,64,768]{2,1,0:T(8,128)(2,1)}) %all-reduce.5.cloned.1.call-update) | async-done | bytes 196624 | tf_op jit(solution)/shard_map/psum | solution.py:39
  388.6 20.9 %subtract_convert_fusion = bf16[2,3072,768]{2,1,0:T(8,128)(2,1)} fusion(f32[2,3072,768]{2,1,0:T(8,128)} %convert_add_fusion, f32[2,64,3072]{2,1,0:T(8,128)} %all-gather.5.cloned.1.call-done, bf16[2,64,768]{2,1,0:T(8,128)(2,1)} %all-reduce.5.cloned.1.call-done), kind=kOutput, calls=%fused_computation.1 | convolution fusion | flops 3633512448 | bytes 30081024 | tf_op jit(solution)/shard_map/lrd,lre->lde/dot_general | solution.py:46
  409.5 3.1 convolution_convert_fusion
  (27 shorter events, 0.4 us)
Async XLA Ops:
  7.2 91.5 %copy-start = (bf16[2,1024,768]{2,1,0:T(8,128)(2,1)S(1)}, bf16[2,1024,768]{2,1,0:T(8,128)(2,1)}, u32[]{:S(2)}) copy-start(bf16[2,1024,768]{2,1,0:T(8,128)(2,1)} %param.4) | copy-start | bytes 9437188
  7.2 91.5 %all-gather.3.cloned.1.call-start = ((), (), s32[]{:S(2)}) async-start(), calls=%async_computation.1 | async-start | bytes 15728640 | tf_op jit(solution)/shard_map/all_gather | solution.py:27
  12.0 105.9 %copy-start.4 = (f32[2,64,768]{2,1,0:T(8,128)S(1)}, f32[2,64,768]{2,1,0:T(8,128)}, u32[]{:S(2)}) copy-start(f32[2,64,768]{2,1,0:T(8,128)} %param.7) | copy-start | bytes 1179652
  12.0 156.6 %reduce-scatter.2.cloned.1.call-start = ((), (), s32[]{:S(2)}) async-start(), calls=%async_computation.2 | async-start | bytes 1966080 | tf_op jit(solution)/shard_map/reduce_scatter | solution.py:33
  140.5 103.4 %all-reduce.3.cloned.1.call-start = ((), (), s32[]{:S(2)}) async-start(), calls=%async_computation.3 | async-start | bytes 786432 | tf_op jit(solution)/shard_map/psum | solution.py:34
  168.7 132.8 %all-gather.5.cloned.1.call-start = ((), (), s32[]{:S(2)}) async-start(), calls=%async_computation.4 | async-start | bytes 1966080 | tf_op jit(solution)/shard_map/all_gather | solution.py:37
  243.9 37.5 %copy-start.2 = (f32[2,64,768]{2,1,0:T(8,128)S(1)}, f32[2,64,768]{2,1,0:T(8,128)}, u32[]{:S(2)}) copy-start(f32[2,64,768]{2,1,0:T(8,128)} %all-reduce.3.cloned.1.call-done) | copy-start | bytes 1179652
  282.6 106.0 %all-reduce.5.cloned.1.call-start = ((), (), s32[]{:S(2)}) async-start(), calls=%async_computation.5 | async-start | bytes 393216 | tf_op jit(solution)/shard_map/psum | solution.py:39
  388.6 20.9 %copy-start.3 = (bf16[2,64,768]{2,1,0:T(8,128)(2,1)S(1)}, bf16[2,64,768]{2,1,0:T(8,128)(2,1)}, u32[]{:S(2)}) copy-start(bf16[2,64,768]{2,1,0:T(8,128)(2,1)} %all-reduce.5.cloned.1.call-done) | copy-start | bytes 589828
  388.6 24.0 %copy-start.1 = (bf16[2,1024,768]{2,1,0:T(8,128)(2,1)S(1)}, bf16[2,1024,768]{2,1,0:T(8,128)(2,1)}, u32[]{:S(2)}) copy-start(bf16[2,1024,768]{2,1,0:T(8,128)(2,1)} %param.4) | copy-start | bytes 9437188
Sparse Core Ops, SparseCore 0:
  12.2 86.4 all-gather.2
  140.6 27.9 reduce-scatter.1
  172.0 71.8 all-reduce.2
  282.8 18.6 all-gather.4
  317.9 70.6 all-reduce.4
where the time goes:
time: 419 us
  waiting for transfers between devices  279 us (67%)
  matrix products  85 us (20%)
  other arithmetic  22 us (5%)
  between operations  13.9 us (3%)
  blocking collectives  10.9 us (3%)
  local copies, waits for them, and re-layouts  7.81 us (2%)
    all_gather x1, waiting for transfers between devices, compress(): lax.all_gather(out_grad, 'tensor', axis=1, tiled=True)  86.6 us
    psum x1, waiting for transfers between devices, compress(): left_part = lax.psum(left_part, 'dp')  75 us
    psum x1, waiting for transfers between devices, compress(): lax.psum(right_terms.astype(jnp.bfloat16), 'dp').astype(jnp.float32)  70.8 us
    reduce_scatter x1, waiting for transfers between devices, compress(): lax.psum_scatter(left_factor, 'tensor', scatter_dimension=2, tiled=True)  28.1 us
    dot_general x1, matrix products, compress(): jnp.einsum('lre,lde->lrd', right_init, moment, precision=lax.Precision.HI...  22.5 us
    dot_general x1, matrix products, compress(): jnp.einsum('lrd,lre->lde', ortho_basis, right_factor / replicas, precisio...  20.9 us
    dot_general x1, matrix products, compress(): jnp.einsum('ltd,lte->lde', lax.all_gather(out_grad, 'tensor', axis=1, til...  19.3 us
    all_gather x1, waiting for transfers between devices, compress(): ortho_basis = lax.all_gather(ortho_part, 'tensor', axis=2, tiled=True)  18.8 us
  transfers between devices with their start and end apart: 5, of which 5 were waited for; matrix products, arithmetic and copies ran while one was open for 0% of the time, Pallas kernels for 0%

commit v1 on v0

--- a/solution.py
+++ b/solution.py
@@ -2,6 +2,18 @@
 import jax.numpy as jnp
 from jax import lax
 from jax.sharding import PartitionSpec as P
+
+
+def product_in_turn(value, axis, dim, term):
+    peers, here = (lax.axis_size(axis), lax.axis_index(axis))
+    downward = [(i, (i - 1) % peers) for i in range(peers)]
+    rows = value.shape[dim]
+    held = value
+    running = term(held, here * rows)
+    for hop in range(1, peers):
+        held = lax.ppermute(held, axis, downward)
+        running = running + term(held, (here + hop) % peers * rows)
+    return running
 
 
 def solve_rows(gram_matrix, left_factor):
@@ -22,11 +34,16 @@
 
 def compress(context, out_grad, error_in, right_init):
     out_width = out_grad.shape[2]
-    moment = jnp.einsum(
-        "ltd,lte->lde",
-        lax.all_gather(out_grad, "tensor", axis=1, tiled=True),
-        context,
-        preferred_element_type=jnp.float32,
+    moment = product_in_turn(
+        out_grad,
+        "tensor",
+        1,
+        lambda own_block, at: jnp.einsum(
+            "ltd,lte->lde",
+            own_block,
+            lax.dynamic_slice_in_dim(context, at, own_block.shape[1], axis=1),
+            preferred_element_type=jnp.float32,
+        ),
     )
     moment = moment + error_in.astype(jnp.float32)
     left_factor = jnp.einsum("lre,lde->lrd", right_init, moment, precision=lax.Precision.HIGHEST)

time: 419 us -> 470 us (1.12)
  matrix products: 85 us -> 123 us
  local copies, waits for them, and re-layouts: 7.81 us -> 30.1 us
  waiting for transfers between devices: 279 us -> 263 us
  starting transfers between devices: 0.2 us -> 6.46 us
    all_gather x1 -> x0, waiting for transfers between devices: 86.6 us -> none  [compress(): lax.all_gather(out_grad, 'tensor', axis=1, tiled=True)]
    ppermute x0 -> x3, waiting for transfers between devices: none -> 69.9 us  [product_in_turn(): held = lax.ppermute(held, axis, downward)]
    dot_general x1 -> x4, matrix products: 19.3 us -> 57.4 us  [compress(): jnp.einsum('ltd,lte->lde', own_block, lax.dynamic_slice_in_dim(context, a...]
    unnamed x11 -> x18, local copies, waits for them, and re-layouts: 4.83 us -> 27.1 us
    dot_general x1, matrix products: 16.3 us -> 22.8 us  [compress(): jnp.einsum('lrd,lde->lre', ortho_basis, moment, precision=lax.Precision.H...]
    ppermute x0 -> x3, starting transfers between devices: none -> 6.3 us  [product_in_turn(): held = lax.ppermute(held, axis, downward)]
    dot_general x1, matrix products: 22.5 us -> 16.5 us  [compress(): jnp.einsum('lre,lde->lrd', right_init, moment, precision=lax.Precision.HI...]
  transfers between devices with their start and end apart: 5 -> 7, of which waited for: 5 -> 6; matrix products, arithmetic and copies ran while one was open for 0% -> 9% of each run, Pallas kernels for 0% -> 0%
where the time goes in v1:
time: 470 us; the launch traced here: 469 us
  waiting for transfers between devices  263 us (56%)
  matrix products  123 us (26%)
  local copies, waits for them, and re-layouts  30.1 us (6%)
  other arithmetic  22 us (5%)
  between operations  13.9 us (3%)
  blocking collectives  10.9 us (2%)
  starting transfers between devices  6.46 us (1%)
    psum x1, waiting for transfers between devices, compress(): left_part = lax.psum(left_part, 'dp')  74.9 us
    psum x1, waiting for transfers between devices, compress(): lax.psum(right_terms.astype(jnp.bfloat16), 'dp').astype(jnp.float32)  70.8 us
    ppermute x3, waiting for transfers between devices, product_in_turn(): held = lax.ppermute(held, axis, downward)  69.9 us
    dot_general x4, matrix products, compress(): jnp.einsum('ltd,lte->lde', own_block, lax.dynamic_slice_in_dim(context, a...  57.4 us
    reduce_scatter x1, waiting for transfers between devices, compress(): lax.psum_scatter(left_factor, 'tensor', scatter_dimension=2, tiled=True)  28.5 us
    unnamed x18, local copies, waits for them, and re-layouts  27.1 us
    dot_general x1, matrix products, compress(): jnp.einsum('lrd,lde->lre', ortho_basis, moment, precision=lax.Precision.H...  22.8 us
    dot_general x1, matrix products, compress(): jnp.einsum('lrd,lre->lde', ortho_basis, right_factor / replicas, precisio...  19.9 us
  transfers between devices with their start and end apart: 7, of which 6 were waited for; matrix products, arithmetic and copies ran while one was open for 9% of the time, Pallas kernels for 0%

profile of v1, /device:TPU:0, one launch (start us, length us, event | category | flops | bytes accessed | tf_op | source)
XLA Modules:
  0.0 468.8 jit_solution(5994183438253462326)
XLA Ops:
  7.2 2.5 collective-permute-start
  9.7 35.1 %collective-permute-done = bf16[2,256,3072]{2,1,0:T(8,128)(2,1)S(1)} collective-permute-done((bf16[2,256,3072]{2,1,0:T(8,128)(2,1)}, bf16[2,256,3072]{2,1,0:T(8,128)(2,1)S(1)}, u32[]{:S(2)}, u32[]{:S(2)}) %collective-permute-start) | collective-permute-done | bytes 3145760 | tf_op jit(solution)/shard_map/ppermute | solution.py:14
  44.8 1.7 copy-done.4
  46.5 1.8 collective-permute-start.1
  48.3 34.8 %collective-permute-done.1 = bf16[2,256,3072]{2,1,0:T(8,128)(2,1)} collective-permute-done((bf16[2,256,3072]{2,1,0:T(8,128)(2,1)S(1)}, bf16[2,256,3072]{2,1,0:T(8,128)(2,1)}, u32[]{:S(2)}, u32[]{:S(2)}) %collective-permute-start.1) | collective-permute-done | bytes 3145760 | tf_op jit(solution)/shard_map/ppermute | solution.py:14
  83.1 2.0 collective-permute-start.2
  85.1 12.6 %copy.24 = bf16[2,3072,768]{1,2,0:T(8,128)(2,1)} copy(bf16[2,3072,768]{2,1,0:T(8,128)(2,1)} %param.6) | data formatting | bytes 18874368 | tf_op args[2]
  97.7 9.8 %fusion.5 = f32[2,768,3072]{2,1,0:T(8,128)} fusion(bf16[2,256,3072]{2,1,0:T(8,128)(2,1)} %param.5, bf16[2,1024,768]{2,1,0:T(8,128)(2,1)S(1)} %copy-done, s32[]{:T(128)S(6)} %select_n.38), kind=kOutput, calls=%fused_computation.11 | convolution fusion | flops 2415919104 | bytes 22806532 | tf_op jit(solution)/shard_map/ltd,lte->lde/dot_general | solution.py:41
  107.5 7.9 %fusion.3 = f32[2,768,3072]{2,1,0:T(8,128)} fusion(bf16[2,256,3072]{2,1,0:T(8,128)(2,1)S(1)} %copy-done.5, bf16[2,1024,768]{2,1,0:T(8,128)(2,1)S(1)} %copy-done, s32[]{:T(128)S(6)} %select_n.40), kind=kOutput, calls=%fused_computation.9 | convolution fusion | flops 2415919104 | bytes 22806532 | tf_op jit(solution)/shard_map/ltd,lte->lde/dot_general | solution.py:41
  115.5 9.6 %fusion.1 = f32[2,768,3072]{2,1,0:T(8,128)} fusion(bf16[2,256,3072]{2,1,0:T(8,128)(2,1)} %collective-permute-done.1, bf16[2,1024,768]{2,1,0:T(8,128)(2,1)S(1)} %copy-done, s32[]{:T(128)S(6)} %select_n.42), kind=kOutput, calls=%fused_computation.7 | convolution fusion | flops 2415919104 | bytes 22806532 | tf_op jit(solution)/shard_map/ltd,lte->lde/dot_general | solution.py:41
  125.1 30.0 %bitcast_add_fusion = f32[2,3072,768]{1,2,0:T(8,128)} fusion(bf16[2,3072,768]{1,2,0:T(8,128)(2,1)} %copy.24, f32[2,768,3072]{2,1,0:T(8,128)} %fusion.1, f32[2,768,3072]{2,1,0:T(8,128)} %fusion.5, f32[2,768,3072]{2,1,0:T(8,128)} %fusion.3, bf16[2,256,3072]{2,1,0:T(8,128)(2,1)} %collective-permute-done.2, bf16[2,1024,768]{2,1,0:T(8,128)(2,1)S(1)} %copy-done, ...), kind=kOutput, calls=%fused_computation.1 | convolution fusion | flops 2439512064 | bytes 88866816 | tf_op jit(solution)/shard_map/ltd,lte->lde/dot_general | solution.py:41
  155.1 16.5 %convolution_bitcast_fusion = f32[2,64,3072]{2,1,0:T(8,128)} fusion(f32[2,3072,768]{1,2,0:T(8,128)} %bitcast_add_fusion, f32[2,64,768]{2,1,0:T(8,128)S(1)} %copy-done.7), kind=kOutput, calls=%fused_computation.3 | convolution fusion | flops 3623878656 | bytes 20840448 | tf_op jit(solution)/shard_map/lre,lde->lrd/dot_general | solution.py:49
  171.7 28.5 %reduce-scatter.2.cloned.1.call-done = f32[2,64,768]{2,1,0:T(8,128)} async-done(((f32[2,64,3072]{2,1,0:T(8,128)}), f32[2,64,768]{2,1,0:T(8,128)}) %reduce-scatter.2.cloned.1.call-update) | async-done | bytes 393232 | tf_op jit(solution)/shard_map/reduce_scatter | solution.py:50
  200.3 74.9 %all-reduce.3.cloned.1.call-done = f32[2,64,768]{2,1,0:T(8,128)} async-done(((f32[2,64,768]{2,1,0:T(8,128)}), f32[2,64,768]{2,1,0:T(8,128)}) %all-reduce.3.cloned.1.call-update) | async-done | bytes 393232 | tf_op jit(solution)/shard_map/psum | solution.py:51
  276.9 10.9 %psum.22 = f32[2,64,64]{1,2,0:T(8,128)S(1)} all-reduce(f32[2,64,64]{1,2,0:T(8,128)S(1)} %fusion.21), channel_id=1, replica_groups=mesh['dp'=8,'tensor'=4] {'tensor'}, use_global_device_ids=true, to_apply=%region_2.3 | all-reduce | flops 8192 | bytes 65536 | tf_op jit(solution)/shard_map/psum | solution.py:52
  287.8 1.9 copy.27
  290.9 11.7 %custom-call.8 = f32[2,64,64]{2,1,0:T(8,128)S(1)} custom-call(f32[2,64,64]{2,1,0:T(8,128)S(1)} %fusion.13), custom_call_target="Cholesky" | custom-call | tf_op jit(solution)/shard_map/jit(cholesky)/cholesky | solution.py:23
  302.9 9.8 %custom-call.9 = f32[2,1,64,64]{2,3,1,0:T(8,128)S(1)} custom-call(f32[2,1,64,64]{3,2,1,0:T(8,128)S(1)} %select_bitcast_fusion), custom_call_target="InvertDiagBlocksLowerTriangular" | custom-call | tf_op jit(solution)/shard_map/vmap(jit(_solve_triangular))/triangular_solve | solution.py:26
  314.1 18.8 %all-gather.2.cloned.1.call-done = f32[2,64,3072]{2,1,0:T(8,128)} async-done(((f32[2,64,768]{2,1,0:T(8,128)}), f32[2,64,3072]{2,1,0:T(8,128)}) %all-gather.2.cloned.1.call-update) | async-done | bytes 1572880 | tf_op jit(solution)/shard_map/all_gather | solution.py:54
  332.9 22.8 %convolution_convert_fusion.1 = bf16[2,64,768]{2,1,0:T(8,128)(2,1)} fusion(f32[2,64,3072]{2,1,0:T(8,128)} %all-gather.2.cloned.1.call-done, f32[2,3072,768]{1,2,0:T(8,128)} %bitcast_add_fusion), kind=kOutput, calls=%fused_computation.5 | convolution fusion | flops 3623976960 | bytes 20643840 | tf_op jit(solution)/shard_map/lrd,lde->lre/dot_general | solution.py:55
  355.7 70.8 %all-reduce.5.cloned.1.call-done = bf16[2,64,768]{2,1,0:T(8,128)(2,1)} async-done(((bf16[2,64,768]{2,1,0:T(8,128)(2,1)}), bf16[2,64,768]{2,1,0:T(8,128)(2,1)}) %all-reduce.5.cloned.1.call-update) | async-done | bytes 196624 | tf_op jit(solution)/shard_map/psum | solution.py:56
  426.5 19.9 %subtract_convert_fusion = bf16[2,3072,768]{1,2,0:T(8,128)(2,1)} fusion(f32[2,3072,768]{1,2,0:T(8,128)} %bitcast_add_fusion, f32[2,64,3072]{2,1,0:T(8,128)S(1)} %copy-done.2, bf16[2,64,768]{2,1,0:T(8,128)(2,1)} %all-reduce.5.cloned.1.call-done), kind=kOutput, calls=%fused_computation.2 | convolution fusion | flops 3633512448 | bytes 30081024 | tf_op jit(solution)/shard_map/lrd,lre->lde/dot_general | solution.py:63
  446.5 12.8 %copy.33 = bf16[2,3072,768]{2,1,0:T(8,128)(2,1)} copy(bf16[2,3072,768]{1,2,0:T(8,128)(2,1)} %subtract_convert_fusion) | data formatting | bytes 18874368
  459.2 3.1 convolution_convert_fusion
  (40 shorter events, 4.7 us)
Async XLA Ops:
  7.2 90.5 %copy-start = (bf16[2,1024,768]{2,1,0:T(8,128)(2,1)S(1)}, bf16[2,1024,768]{2,1,0:T(8,128)(2,1)}, u32[]{:S(2)}) copy-start(bf16[2,1024,768]{2,1,0:T(8,128)(2,1)} %param.4) | copy-start | bytes 9437188
  7.2 192.9 %reduce-scatter.2.cloned.1.call-start = ((), (), s32[]{:S(2)}) async-start(), calls=%async_computation.1 | async-start | bytes 1966080 | tf_op jit(solution)/shard_map/reduce_scatter | solution.py:50
  7.2 37.6 %collective-permute-start = (bf16[2,256,3072]{2,1,0:T(8,128)(2,1)}, bf16[2,256,3072]{2,1,0:T(8,128)(2,1)S(1)}, u32[]{:S(2)}, u32[]{:S(2)}) collective-permute-start(bf16[2,256,3072]{2,1,0:T(8,128)(2,1)} %param.5), channel_id=1, source_target_pairs={{0,3},{1,0},{2,1},{3,2},{4,7},{5,4},{6,5},{7,6},{8,11},{9,8},{10,9... | collective-permute-start | bytes 9437192 | tf_op jit(solution)/shard_map/ppermute | solution.py:14
  44.8 1.7 copy-start.4
  46.5 36.6 %collective-permute-start.1 = (bf16[2,256,3072]{2,1,0:T(8,128)(2,1)S(1)}, bf16[2,256,3072]{2,1,0:T(8,128)(2,1)}, u32[]{:S(2)}, u32[]{:S(2)}) collective-permute-start(bf16[2,256,3072]{2,1,0:T(8,128)(2,1)S(1)} %collective-permute-done), channel_id=1, source_target_pairs={{0,3},{1,0},{2,1},{3,2},{4,7},{5,4},{6,5},{7,6},{8,11},{9,8},{10,9... | collective-permute-start | bytes 9437192 | tf_op jit(solution)/shard_map/ppermute | solution.py:14
  83.1 42.0 %collective-permute-start.2 = (bf16[2,256,3072]{2,1,0:T(8,128)(2,1)}, bf16[2,256,3072]{2,1,0:T(8,128)(2,1)}, u32[]{:S(2)}, u32[]{:S(2)}) collective-permute-start(bf16[2,256,3072]{2,1,0:T(8,128)(2,1)} %collective-permute-done.1), channel_id=1, source_target_pairs={{0,3},{1,0},{2,1},{3,2},{4,7},{5,4},{6,5},{7,6},{8,11},{9,8},{10,9... | collective-permute-start | bytes 9437192 | tf_op jit(solution)/shard_map/ppermute | solution.py:14
  97.7 9.8 %copy-start.5 = (bf16[2,256,3072]{2,1,0:T(8,128)(2,1)S(1)}, bf16[2,256,3072]{2,1,0:T(8,128)(2,1)}, u32[]{:S(2)}) copy-start(bf16[2,256,3072]{2,1,0:T(8,128)(2,1)} %copy-done.4) | copy-start | bytes 9437188
  125.1 30.0 %copy-start.7 = (f32[2,64,768]{2,1,0:T(8,128)S(1)}, f32[2,64,768]{2,1,0:T(8,128)}, u32[]{:S(2)}) copy-start(f32[2,64,768]{2,1,0:T(8,128)} %param.7) | copy-start | bytes 1179652
  171.6 103.7 %all-reduce.3.cloned.1.call-start = ((), (), s32[]{:S(2)}) async-start(), calls=%async_computation.2 | async-start | bytes 786432 | tf_op jit(solution)/shard_map/psum | solution.py:51
  200.1 132.7 %all-gather.2.cloned.1.call-start = ((), (), s32[]{:S(2)}) async-start(), calls=%async_computation.3 | async-start | bytes 1966080 | tf_op jit(solution)/shard_map/all_gather | solution.py:54
  275.3 37.5 %copy-start.3 = (f32[2,64,768]{2,1,0:T(8,128)S(1)}, f32[2,64,768]{2,1,0:T(8,128)}, u32[]{:S(2)}) copy-start(f32[2,64,768]{2,1,0:T(8,128)} %all-reduce.3.cloned.1.call-done) | copy-start | bytes 1179652
  314.1 112.5 %all-reduce.5.cloned.1.call-start = ((), (), s32[]{:S(2)}) async-start(), calls=%async_computation.4 | async-start | bytes 393216 | tf_op jit(solution)/shard_map/psum | solution.py:56
  332.9 93.7 %copy-start.2 = (f32[2,64,3072]{2,1,0:T(8,128)S(1)}, f32[2,64,3072]{2,1,0:T(8,128)}, u32[]{:S(2)}) copy-start(f32[2,64,3072]{2,1,0:T(8,128)} %all-gather.2.cloned.1.call-done) | copy-start | bytes 4718596
  446.5 12.8 %copy-start.6 = (bf16[2,64,768]{2,1,0:T(8,128)(2,1)S(1)}, bf16[2,64,768]{2,1,0:T(8,128)(2,1)}, u32[]{:S(2)}) copy-start(bf16[2,64,768]{2,1,0:T(8,128)(2,1)} %all-reduce.5.cloned.1.call-done) | copy-start | bytes 589828
  446.5 15.8 %copy-start.1 = (bf16[2,1024,768]{2,1,0:T(8,128)(2,1)S(1)}, bf16[2,1024,768]{2,1,0:T(8,128)(2,1)}, u32[]{:S(2)}) copy-start(bf16[2,1024,768]{2,1,0:T(8,128)(2,1)} %param.4) | copy-start | bytes 9437188
Sparse Core Ops, SparseCore 0:
  171.7 28.3 reduce-scatter.1
  203.5 71.7 all-reduce.2
  314.2 18.6 all-gather.1
  355.8 70.6 all-reduce.4
